TPU v7x, 32 devices: a whole 2x2x4 slice. The times are simulated.
32 devices in a mesh: tm: 4 (over z), row: 2 (over core), col: 4 (over y, x).
Axes of the slice: x: 2, y: 2, z: 4, core: 2. Of those that a mesh axis runs over, the one named last changes fastest.
Arguments:
- features: bfloat16 [8, 32, 128, 128], P('tm', 'row', 'col'), may hold values from -65 to 65
- conv_first: bfloat16 [3, 3, 3, 128, 128], replicated, may hold values from -0.109375 to 0.109375
- conv_second: bfloat16 [3, 3, 3, 128, 128], replicated, may hold values from -0.109375 to 0.109375
- out_grad: bfloat16 [8, 32, 128, 128], P('tm', 'row', 'col'), may hold values from -6 to 6
Outputs:
- result: bfloat16 [8, 32, 128, 128], P('tm', 'row', 'col')
- feature_grad: bfloat16 [8, 32, 128, 128], P('tm', 'row', 'col')
- first_grad: bfloat16 [3, 3, 3, 128, 128], replicated
- second_grad: bfloat16 [3, 3, 3, 128, 128], replicated
All inputs are finite; a program needn't handle non-finite values.
Results may differ from a plain program's by a relative error of at most 0.0068.
Values may be sent and summed in bfloat16 or wider, within the bound.
No kernel may reach another device: no remote copies, remote signals or barrier semaphores. Data moves between devices by JAX's collectives and lax.ppermute only.
A program may use at most 64 MiB of HBM per device.

v0:
```python
import math
import jax
import jax.numpy as jnp
from jax import lax
from jax.sharding import PartitionSpec as P

GROUPS = 32
EPSILON = 1e-06
NUMBERS = ("NDHWC", "DHWIO", "NDHWC")
SWAPPED = ("CDHWN", "DHWIO", "CDHWN")


def extended(cells, sides, width):
    for axis, dim in sides:
        count = lax.axis_size(axis)
        ends = count - 1
        head = lax.slice_in_dim(cells, 0, width, axis=dim)
        tail = lax.slice_in_dim(cells, cells.shape[dim] - width, cells.shape[dim], axis=dim)
        cells = jnp.concatenate(
            [
                lax.ppermute(tail, axis, [(i, (i + 1) % count) for i in range(ends)]),
                cells,
                lax.ppermute(head, axis, [((i + 1) % count, i) for i in range(ends)]),
            ],
            axis=dim,
        )
    return cells


def passed_along(shard, axis, by):
    peers = lax.axis_size(axis)
    pairs = [(i, i + by) for i in range(peers) if 0 <= i + by < peers]
    return lax.ppermute(shard, axis, pairs)


def conv_valid(window, kernel):
    return lax.conv_general_dilated(
        window[None],
        kernel,
        (1, 1, 1),
        "VALID",
        dimension_numbers=NUMBERS,
        preferred_element_type=jnp.float32,
    )[0]


def flipped(kernel):
    return jnp.transpose(jnp.flip(kernel, (0, 1, 2)), (0, 1, 2, 4, 3))


def window(values, step):
    rimmed = extended(values, (("row", 1), ("col", 2)), 1)
    if step > 0:
        piece = rimmed[-2:]
    else:
        piece = rimmed[:2]
    neighbour = passed_along(piece, "tm", step)
    if step > 0:
        return jnp.concatenate([neighbour, rimmed], 0)
    return jnp.concatenate([rimmed, neighbour], 0)


def group_sum(values):
    per_group = values.shape[3] // GROUPS
    return values.sum((1, 2)).reshape(values.shape[0], GROUPS, per_group).sum(2)


def widen(stat, per_group):
    return jnp.repeat(stat, per_group, axis=1)[:, None, None, :]


def tile_count(values):
    return (
        values.shape[1]
        * values.shape[2]
        * lax.axis_size("row")
        * lax.axis_size("col")
        * (values.shape[3] // GROUPS)
    )


def norm_act(raw):
    values = raw.astype(jnp.float32)
    per_group = values.shape[3] // GROUPS
    count = tile_count(values)
    group_mean = lax.psum(group_sum(values), ("row", "col")) / count
    centred = values - widen(group_mean, per_group)
    spread = lax.psum(group_sum(centred * centred), ("row", "col")) / count
    inv_std = widen(lax.rsqrt(spread + EPSILON), per_group)
    normed = centred * inv_std
    return ((normed * jax.nn.sigmoid(normed)).astype(jnp.bfloat16), normed, inv_std)


def norm_back(grad_act, normed, inv_std):
    per_group = normed.shape[3] // GROUPS
    count = tile_count(normed)
    sigmoid_z = jax.nn.sigmoid(normed)
    grad_norm = grad_act * sigmoid_z * (1.0 + normed * (1.0 - sigmoid_z))
    first_total, second_total = lax.psum(
        (group_sum(grad_norm), group_sum(grad_norm * normed)), ("row", "col")
    )
    first_mean = widen(first_total / count, per_group)
    second_mean = widen(second_total / count, per_group)
    return inv_std * (grad_norm - first_mean - normed * second_mean)


def weight_grad(padded, grad):
    summed = lax.conv_general_dilated(
        padded[None],
        grad[:, :, :, None, :],
        (1, 1, 1),
        "VALID",
        dimension_numbers=SWAPPED,
        preferred_element_type=jnp.float32,
    )
    return jnp.transpose(summed, (1, 2, 3, 4, 0))


def on_device(features, conv_first, conv_second, out_grad):
    cells = (
        features.shape[0]
        * features.shape[1]
        * features.shape[2]
        * lax.axis_size("tm")
        * lax.axis_size("row")
        * lax.axis_size("col")
    )
    factor = 1.0 / math.sqrt(cells)
    act_first, norm_first, std_first = norm_act(features)
    pad_first = window(act_first, 1)
    hidden = conv_valid(pad_first, conv_first).astype(jnp.bfloat16)
    act_second, norm_second, std_second = norm_act(hidden)
    pad_second = window(act_second, 1)
    branch = conv_valid(pad_second, conv_second)
    result = (features.astype(jnp.float32) + branch).astype(jnp.bfloat16)
    grad_window = window(out_grad, -1)
    second_term = weight_grad(pad_second, out_grad)
    grad_act2 = conv_valid(grad_window, flipped(conv_second))
    hidden_grad = norm_back(grad_act2, norm_second, std_second).astype(jnp.bfloat16)
    hidden_window = window(hidden_grad, -1)
    grad_act1 = conv_valid(hidden_window, flipped(conv_first))
    first_term = weight_grad(pad_first, hidden_grad)
    feature_grad = (
        out_grad.astype(jnp.float32) + norm_back(grad_act1, norm_first, std_first)
    ).astype(jnp.bfloat16)
    first_total, second_total = lax.psum((first_term, second_term), ("tm", "row", "col"))
    first_grad = (first_total * factor).astype(jnp.bfloat16)
    second_grad = (second_total * factor).astype(jnp.bfloat16)
    return (result, feature_grad, first_grad, second_grad)


def solution(mesh):
    in_specs = (P("tm", "row", "col", None), P(), P(), P("tm", "row", "col", None))
    out_specs = (P("tm", "row", "col", None), P("tm", "row", "col", None), P(), P())
    return jax.shard_map(
        on_device, mesh=mesh, in_specs=in_specs, out_specs=out_specs, check_vma=False
    )
```

profile of v0, /device:TPU:0, one launch (start us, length us, event | category | flops | bytes accessed | tf_op | source)
XLA Modules:
  0.0 334.4 jit_solution(3689381599951502855)
XLA Ops:
  8.6 15.8 %psum.70 = f32[2,32]{1,0:T(2,128)S(1)} all-reduce(f32[2,32]{1,0:T(2,128)S(1)} %reduce_sum.145), channel_id=1, replica_groups=mesh['tm'=4,'row'=2,'col'=4] {'row','col'}, use_global_device_ids=true, to_apply=%region_2.0 | all-reduce | flops 64 | bytes 512 | tf_op jit(solution)/shard_map/psum | solution.py:86
  25.8 14.2 %psum.71 = f32[2,32]{1,0:T(2,128)S(1)} all-reduce(f32[2,32]{1,0:T(2,128)S(1)} %reduce_sum.147), channel_id=1, replica_groups=mesh['tm'=4,'row'=2,'col'=4] {'row','col'}, use_global_device_ids=true, to_apply=%region_5.0 | all-reduce | flops 64 | bytes 512 | tf_op jit(solution)/shard_map/psum | solution.py:88
  43.3 3.0 collective-permute-start
  51.0 4.8 %collective-permute-start.2 = (bf16[2,18,1,128]{3,1,2,0:T(8,128)(2,1)S(1)}, bf16[2,18,1,128]{3,1,2,0:T(8,128)(2,1)S(1)}, u32[]{:S(2)}, u32[]{:S(2)}) collective-permute-start(bf16[2,18,1,128]{3,1,2,0:T(8,128)(2,1)S(1)} %get-tuple-element.30), channel_id=1, source_target_pairs={{0,1},{1,2},{2,3},{4,5},{5,6},{6,7},{8,9},{9,10},{10,11},{12,13},{... | collective-permute-start | bytes 27656 | tf_op jit(solution)/shard_map/ppermute | solution.py:21
  57.4 3.5 %collective-permute-start.4 = (bf16[2,18,34,128]{3,1,2,0:T(8,128)(2,1)S(1)}, bf16[2,18,34,128]{3,1,2,0:T(8,128)(2,1)S(1)}, u32[]{:S(2)}, u32[]{:S(2)}) collective-permute-start(bf16[2,18,34,128]{3,1,2,0:T(8,128)(2,1)S(1)} %pad_maximum_fusion), channel_id=1, source_target_pairs={{0,8},{8,16},{16,24},{1,9},{9,17},{17,25},{2,10},{10,18},{18,26},{... | collective-permute-start | bytes 940040 | tf_op jit(solution)/shard_map/ppermute | solution.py:33
  62.2 5.4 %collective-permute-start.12 = (bf16[2,18,1,128]{3,2,1,0:T(2,128)(2,1)S(1)}, bf16[2,18,1,128]{3,2,1,0:T(2,128)(2,1)S(1)}, u32[]{:S(2)}, u32[]{:S(2)}) collective-permute-start(bf16[2,18,1,128]{3,2,1,0:T(2,128)(2,1)S(1)} %get-tuple-element.32), channel_id=1, source_target_pairs={{0,1},{1,2},{2,3},{4,5},{5,6},{6,7},{8,9},{9,10},{10,11},{12,13},{... | collective-permute-start | bytes 27656 | tf_op jit(solution)/shard_map/ppermute | solution.py:21
  72.5 2.5 select_reduce_fusion
  75.3 17.4 %psum.72 = f32[2,32]{1,0:T(2,128)S(1)} all-reduce(f32[2,32]{1,0:T(2,128)S(1)} %reduce_sum.149), channel_id=1, replica_groups=mesh['tm'=4,'row'=2,'col'=4] {'row','col'}, use_global_device_ids=true, to_apply=%region_8.0 | all-reduce | flops 64 | bytes 512 | tf_op jit(solution)/shard_map/psum | solution.py:86
  93.1 14.5 %psum.73 = f32[2,32]{1,0:T(2,128)S(1)} all-reduce(f32[2,32]{1,0:T(2,128)S(1)} %reduce_sum.151), channel_id=1, replica_groups=mesh['tm'=4,'row'=2,'col'=4] {'row','col'}, use_global_device_ids=true, to_apply=%region_11.0 | all-reduce | flops 64 | bytes 512 | tf_op jit(solution)/shard_map/psum | solution.py:88
  109.5 2.5 convolution_select_fusion.1
  112.8 14.7 %all-reduce.2 = (f32[2,32]{1,0:T(2,128)S(1)}, f32[2,32]{1,0:T(2,128)S(1)}) all-reduce(f32[2,32]{1,0:T(2,128)S(1)} %reduce_sum.155, f32[2,32]{1,0:T(2,128)S(1)} %reduce_sum.153), channel_id=1, replica_groups=mesh['tm'=4,'row'=2,'col'=4] {'row','col'}, use_global_device_ids=true, to_apply=%region_17.18 | all-reduce | flops 128 | bytes 1024 | tf_op jit(solution)/shard_map/psum | solution.py:99
  129.7 3.0 collective-permute-start.15
  134.1 3.0 collective-permute-start.5
  139.3 4.5 %collective-permute-start.7 = (bf16[2,18,1,128]{3,1,2,0:T(8,128)(2,1)S(1)}, bf16[2,18,1,128]{3,1,2,0:T(8,128)(2,1)S(1)}, u32[]{:S(2)}, u32[]{:S(2)}) collective-permute-start(bf16[2,18,1,128]{3,1,2,0:T(8,128)(2,1)S(1)} %get-tuple-element.28), channel_id=1, source_target_pairs={{0,1},{1,2},{2,3},{4,5},{5,6},{6,7},{8,9},{9,10},{10,11},{12,13},{... | collective-permute-start | bytes 27656 | tf_op jit(solution)/shard_map/ppermute | solution.py:21
  145.8 5.8 %collective-permute-start.17 = (bf16[2,18,1,128]{3,1,2,0:T(8,128)(2,1)}, bf16[2,18,1,128]{3,1,2,0:T(8,128)(2,1)}, u32[]{:S(2)}, u32[]{:S(2)}) collective-permute-start(bf16[2,18,1,128]{3,1,2,0:T(8,128)(2,1)} %get-tuple-element.26), channel_id=1, source_target_pairs={{0,1},{1,2},{2,3},{4,5},{5,6},{6,7},{8,9},{9,10},{10,11},{12,13},{... | collective-permute-start | bytes 27656 | tf_op jit(solution)/shard_map/ppermute | solution.py:21
  152.6 5.5 %collective-permute-start.9 = (bf16[2,18,34,128]{3,1,2,0:T(8,128)(2,1)}, bf16[2,18,34,128]{3,1,2,0:T(8,128)(2,1)}, u32[]{:S(2)}, u32[]{:S(2)}) collective-permute-start(bf16[2,18,34,128]{3,1,2,0:T(8,128)(2,1)} %pad_maximum_fusion.1), channel_id=1, source_target_pairs={{0,8},{8,16},{16,24},{1,9},{9,17},{17,25},{2,10},{10,18},{18,26},{... | collective-permute-start | bytes 940040 | tf_op jit(solution)/shard_map/ppermute | solution.py:33
  158.1 9.0 %fusion.6 = f32[3,3,3,128,128]{4,3,2,1,0:T(8,128)} fusion(bf16[1,4,18,34,128]{4,2,3,1,0:T(8,128)(2,1)S(1)} %copy-done.11, bf16[2,16,32,1,128]{4,1,2,0,3:T(8,128)(2,1)S(1)} %fusion.67), kind=kOutput, calls=%fused_computation.9 | convolution fusion | flops 905969664 | bytes 2658304 | tf_op jit(solution)/shard_map/transpose | solution.py:116
  170.5 2.3 fusion.89
  172.8 9.0 %fusion.4 = f32[3,3,3,128,128]{4,3,2,1,0:T(8,128)} fusion(bf16[1,4,18,34,128]{4,2,3,1,0:T(8,128)(2,1)S(1)} %get-tuple-element.20, bf16[2,16,32,1,128]{4,2,1,0,3:T(8,128)(2,1)S(1)} %bitcast.93), kind=kOutput, calls=%fused_computation.7 | convolution fusion | flops 905969664 | bytes 2658304 | tf_op jit(solution)/shard_map/transpose | solution.py:116
  184.7 2.5 convolution_select_fusion
  188.1 15.5 %all-reduce.1 = (f32[2,32]{1,0:T(2,128)S(1)}, f32[2,32]{1,0:T(2,128)S(1)}) all-reduce(f32[2,32]{1,0:T(2,128)S(1)} %reduce_sum.159, f32[2,32]{1,0:T(2,128)S(1)} %reduce_sum.157), channel_id=1, replica_groups=mesh['tm'=4,'row'=2,'col'=4] {'row','col'}, use_global_device_ids=true, to_apply=%region_23.24 | all-reduce | flops 128 | bytes 1024 | tf_op jit(solution)/shard_map/psum | solution.py:99
  205.2 2.5 convolution_select_fusion.2
  209.6 114.0 %all-reduce.5.cloned.1.call-done = (f32[3,3,3,128,128]{4,3,2,1,0:T(8,128)}, f32[3,3,3,128,128]{4,3,2,1,0:T(8,128)}) async-done(((f32[3,3,3,128,128]{4,3,2,1,0:T(8,128)}, f32[3,3,3,128,128]{4,3,2,1,0:T(8,128)}), (f32[3,3,3,128,128]{4,3,2,1,0:T(8,128)}, f32[3,3,3,128,128]{4,3,2,1,0:T(8,128)})) %all-reduce.5.cloned.1.call-update) | async-done | bytes 3538960 | tf_op jit(solution)/shard_map/psum | solution.py:146
  323.6 2.8 multiply_convert_fusion.1
  (176 shorter events, 41.8 us)
Async XLA Ops:
  7.2 65.1 %copy-start = (bf16[3,3,3,128,128]{4,3,2,1,0:T(8,128)(2,1)S(1)}, bf16[3,3,3,128,128]{4,3,2,1,0:T(8,128)(2,1)}, u32[]{:S(2)}) copy-start(bf16[3,3,3,128,128]{4,3,2,1,0:T(8,128)(2,1)} %param.5) | copy-start | bytes 2654212
  7.2 48.6 %copy-start.9 = (bf16[2,16,32,128]{3,2,1,0:T(8,128)(2,1)S(1)}, bf16[2,16,32,128]{3,2,1,0:T(8,128)(2,1)}, u32[]{:S(2)}) copy-start(bf16[2,16,32,128]{3,2,1,0:T(8,128)(2,1)} %param.7) | copy-start | bytes 786436
  7.2 316.4 %all-reduce.5.cloned.1.call-start = ((), (), s32[]{:S(2)}) async-start(), calls=%async_computation | async-start | bytes 7077888 | tf_op jit(solution)/shard_map/psum | solution.py:146
  42.0 7.7 %collective-permute-start.1 = (bf16[2,1,32,128]{3,1,2,0:T(2,128)(2,1)S(1)}, bf16[2,1,32,128]{3,1,2,0:T(2,128)(2,1)S(1)}, u32[]{:S(2)}, u32[]{:S(2)}) collective-permute-start(bf16[2,1,32,128]{3,1,2,0:T(2,128)(2,1)S(1)} %get-tuple-element.43), channel_id=1, source_target_pairs={{4,0},{5,1},{6,2},{7,3},{12,8},{13,9},{14,10},{15,11},{20,16},{21,... | collective-permute-start | bytes 49160 | tf_op jit(solution)/shard_map/ppermute | solution.py:23
  43.3 6.4 %collective-permute-start = (bf16[2,1,32,128]{3,1,2,0:T(2,128)(2,1)S(1)}, bf16[2,1,32,128]{3,1,2,0:T(2,128)(2,1)S(1)}, u32[]{:S(2)}, u32[]{:S(2)}) collective-permute-start(bf16[2,1,32,128]{3,1,2,0:T(2,128)(2,1)S(1)} %get-tuple-element.42), channel_id=1, source_target_pairs={{0,4},{1,5},{2,6},{3,7},{8,12},{9,13},{10,14},{11,15},{16,20},{17,... | collective-permute-start | bytes 49160 | tf_op jit(solution)/shard_map/ppermute | solution.py:21
  47.0 8.8 %collective-permute-start.10 = (bf16[2,1,32,128]{3,2,1,0:T(8,128)(2,1)S(1)}, bf16[2,1,32,128]{3,2,1,0:T(8,128)(2,1)S(1)}, u32[]{:S(2)}, u32[]{:S(2)}) collective-permute-start(bf16[2,1,32,128]{3,2,1,0:T(8,128)(2,1)S(1)} %get-tuple-element.39), channel_id=1, source_target_pairs={{0,4},{1,5},{2,6},{3,7},{8,12},{9,13},{10,14},{11,15},{16,20},{17,... | collective-permute-start | bytes 49160 | tf_op jit(solution)/shard_map/ppermute | solution.py:21
  48.3 7.5 %collective-permute-start.11 = (bf16[2,1,32,128]{3,2,1,0:T(8,128)(2,1)S(1)}, bf16[2,1,32,128]{3,2,1,0:T(8,128)(2,1)S(1)}, u32[]{:S(2)}, u32[]{:S(2)}) collective-permute-start(bf16[2,1,32,128]{3,2,1,0:T(8,128)(2,1)S(1)} %get-tuple-element.38), channel_id=1, source_target_pairs={{4,0},{5,1},{6,2},{7,3},{12,8},{13,9},{14,10},{15,11},{20,16},{21,... | collective-permute-start | bytes 49160 | tf_op jit(solution)/shard_map/ppermute | solution.py:23
  49.7 6.2 %collective-permute-start.3 = (bf16[2,18,1,128]{3,1,2,0:T(8,128)(2,1)S(1)}, bf16[2,18,1,128]{3,1,2,0:T(8,128)(2,1)S(1)}, u32[]{:S(2)}, u32[]{:S(2)}) collective-permute-start(bf16[2,18,1,128]{3,1,2,0:T(8,128)(2,1)S(1)} %get-tuple-element.31), channel_id=1, source_target_pairs={{1,0},{2,1},{3,2},{5,4},{6,5},{7,6},{9,8},{10,9},{11,10},{13,12},{... | collective-permute-start | bytes 27656 | tf_op jit(solution)/shard_map/ppermute | solution.py:23
  51.0 6.2 %collective-permute-start.2 = (bf16[2,18,1,128]{3,1,2,0:T(8,128)(2,1)S(1)}, bf16[2,18,1,128]{3,1,2,0:T(8,128)(2,1)S(1)}, u32[]{:S(2)}, u32[]{:S(2)}) collective-permute-start(bf16[2,18,1,128]{3,1,2,0:T(8,128)(2,1)S(1)} %get-tuple-element.30), channel_id=1, source_target_pairs={{0,1},{1,2},{2,3},{4,5},{5,6},{6,7},{8,9},{9,10},{10,11},{12,13},{... | collective-permute-start | bytes 27656 | tf_op jit(solution)/shard_map/ppermute | solution.py:21
  57.4 13.2 %collective-permute-start.4 = (bf16[2,18,34,128]{3,1,2,0:T(8,128)(2,1)S(1)}, bf16[2,18,34,128]{3,1,2,0:T(8,128)(2,1)S(1)}, u32[]{:S(2)}, u32[]{:S(2)}) collective-permute-start(bf16[2,18,34,128]{3,1,2,0:T(8,128)(2,1)S(1)} %pad_maximum_fusion), channel_id=1, source_target_pairs={{0,8},{8,16},{16,24},{1,9},{9,17},{17,25},{2,10},{10,18},{18,26},{... | collective-permute-start | bytes 940040 | tf_op jit(solution)/shard_map/ppermute | solution.py:33
  60.9 6.8 %collective-permute-start.13 = (bf16[2,18,1,128]{3,2,1,0:T(2,128)(2,1)S(1)}, bf16[2,18,1,128]{3,2,1,0:T(2,128)(2,1)S(1)}, u32[]{:S(2)}, u32[]{:S(2)}) collective-permute-start(bf16[2,18,1,128]{3,2,1,0:T(2,128)(2,1)S(1)} %get-tuple-element.33), channel_id=1, source_target_pairs={{1,0},{2,1},{3,2},{5,4},{6,5},{7,6},{9,8},{10,9},{11,10},{13,12},{... | collective-permute-start | bytes 27656 | tf_op jit(solution)/shard_map/ppermute | solution.py:23
  62.2 6.9 %collective-permute-start.12 = (bf16[2,18,1,128]{3,2,1,0:T(2,128)(2,1)S(1)}, bf16[2,18,1,128]{3,2,1,0:T(2,128)(2,1)S(1)}, u32[]{:S(2)}, u32[]{:S(2)}) collective-permute-start(bf16[2,18,1,128]{3,2,1,0:T(2,128)(2,1)S(1)} %get-tuple-element.32), channel_id=1, source_target_pairs={{0,1},{1,2},{2,3},{4,5},{5,6},{6,7},{8,9},{9,10},{10,11},{12,13},{... | collective-permute-start | bytes 27656 | tf_op jit(solution)/shard_map/ppermute | solution.py:21
  69.3 38.5 %collective-permute-start.14 = (bf16[2,18,34,128]{3,2,1,0:T(8,128)(2,1)S(1)}, bf16[2,18,34,128]{3,2,1,0:T(8,128)(2,1)S(1)}, u32[]{:S(2)}, u32[]{:S(2)}) collective-permute-start(bf16[2,18,34,128]{3,2,1,0:T(8,128)(2,1)S(1)} %pad_maximum_fusion.3), channel_id=1, source_target_pairs={{8,0},{16,8},{24,16},{9,1},{17,9},{25,17},{10,2},{18,10},{26,18},{... | collective-permute-start | bytes 940040 | tf_op jit(solution)/shard_map/ppermute | solution.py:33
  128.2 29.9 %copy-start.5 = (bf16[2,16,32,128]{3,1,2,0:T(8,128)(2,1)}, bf16[2,16,32,128]{3,1,2,0:T(8,128)(2,1)S(1)}, u32[]{:S(2)}) copy-start(bf16[2,16,32,128]{3,1,2,0:T(8,128)(2,1)S(1)} %get-tuple-element.25) | copy-start | bytes 786436
  128.3 15.6 %collective-permute-start.16 = (bf16[2,1,32,128]{3,1,2,0:T(2,128)(2,1)S(1)}, bf16[2,1,32,128]{3,1,2,0:T(2,128)(2,1)S(1)}, u32[]{:S(2)}, u32[]{:S(2)}) collective-permute-start(bf16[2,1,32,128]{3,1,2,0:T(2,128)(2,1)S(1)} %get-tuple-element.37), channel_id=1, source_target_pairs={{4,0},{5,1},{6,2},{7,3},{12,8},{13,9},{14,10},{15,11},{20,16},{21,... | collective-permute-start | bytes 49160 | tf_op jit(solution)/shard_map/ppermute | solution.py:23
  129.7 14.2 %collective-permute-start.15 = (bf16[2,1,32,128]{3,1,2,0:T(2,128)(2,1)S(1)}, bf16[2,1,32,128]{3,1,2,0:T(2,128)(2,1)S(1)}, u32[]{:S(2)}, u32[]{:S(2)}) collective-permute-start(bf16[2,1,32,128]{3,1,2,0:T(2,128)(2,1)S(1)} %get-tuple-element.36), channel_id=1, source_target_pairs={{0,4},{1,5},{2,6},{3,7},{8,12},{9,13},{10,14},{11,15},{16,20},{17,... | collective-permute-start | bytes 49160 | tf_op jit(solution)/shard_map/ppermute | solution.py:21
  132.8 4.7 %collective-permute-start.6 = (bf16[2,1,32,128]{3,1,2,0:T(2,128)(2,1)S(1)}, bf16[2,1,32,128]{3,1,2,0:T(2,128)(2,1)S(1)}, u32[]{:S(2)}, u32[]{:S(2)}) collective-permute-start(bf16[2,1,32,128]{3,1,2,0:T(2,128)(2,1)S(1)} %get-tuple-element.41), channel_id=1, source_target_pairs={{4,0},{5,1},{6,2},{7,3},{12,8},{13,9},{14,10},{15,11},{20,16},{21,... | collective-permute-start | bytes 49160 | tf_op jit(solution)/shard_map/ppermute | solution.py:23
  134.1 3.9 %collective-permute-start.5 = (bf16[2,1,32,128]{3,1,2,0:T(2,128)(2,1)S(1)}, bf16[2,1,32,128]{3,1,2,0:T(2,128)(2,1)S(1)}, u32[]{:S(2)}, u32[]{:S(2)}) collective-permute-start(bf16[2,1,32,128]{3,1,2,0:T(2,128)(2,1)S(1)} %get-tuple-element.40), channel_id=1, source_target_pairs={{0,4},{1,5},{2,6},{3,7},{8,12},{9,13},{10,14},{11,15},{16,20},{17,... | collective-permute-start | bytes 49160 | tf_op jit(solution)/shard_map/ppermute | solution.py:21
  138.0 13.6 %collective-permute-start.8 = (bf16[2,18,1,128]{3,1,2,0:T(8,128)(2,1)S(1)}, bf16[2,18,1,128]{3,1,2,0:T(8,128)(2,1)S(1)}, u32[]{:S(2)}, u32[]{:S(2)}) collective-permute-start(bf16[2,18,1,128]{3,1,2,0:T(8,128)(2,1)S(1)} %get-tuple-element.29), channel_id=1, source_target_pairs={{1,0},{2,1},{3,2},{5,4},{6,5},{7,6},{9,8},{10,9},{11,10},{13,12},{... | collective-permute-start | bytes 27656 | tf_op jit(solution)/shard_map/ppermute | solution.py:23
  139.3 12.3 %collective-permute-start.7 = (bf16[2,18,1,128]{3,1,2,0:T(8,128)(2,1)S(1)}, bf16[2,18,1,128]{3,1,2,0:T(8,128)(2,1)S(1)}, u32[]{:S(2)}, u32[]{:S(2)}) collective-permute-start(bf16[2,18,1,128]{3,1,2,0:T(8,128)(2,1)S(1)} %get-tuple-element.28), channel_id=1, source_target_pairs={{0,1},{1,2},{2,3},{4,5},{5,6},{6,7},{8,9},{9,10},{10,11},{12,13},{... | collective-permute-start | bytes 27656 | tf_op jit(solution)/shard_map/ppermute | solution.py:21
  144.5 22.6 %collective-permute-start.18 = (bf16[2,18,1,128]{3,1,2,0:T(8,128)(2,1)}, bf16[2,18,1,128]{3,1,2,0:T(8,128)(2,1)}, u32[]{:S(2)}, u32[]{:S(2)}) collective-permute-start(bf16[2,18,1,128]{3,1,2,0:T(8,128)(2,1)} %get-tuple-element.27), channel_id=1, source_target_pairs={{1,0},{2,1},{3,2},{5,4},{6,5},{7,6},{9,8},{10,9},{11,10},{13,12},{... | collective-permute-start | bytes 27656 | tf_op jit(solution)/shard_map/ppermute | solution.py:23
  145.8 21.3 %collective-permute-start.17 = (bf16[2,18,1,128]{3,1,2,0:T(8,128)(2,1)}, bf16[2,18,1,128]{3,1,2,0:T(8,128)(2,1)}, u32[]{:S(2)}, u32[]{:S(2)}) collective-permute-start(bf16[2,18,1,128]{3,1,2,0:T(8,128)(2,1)} %get-tuple-element.26), channel_id=1, source_target_pairs={{0,1},{1,2},{2,3},{4,5},{5,6},{6,7},{8,9},{9,10},{10,11},{12,13},{... | collective-permute-start | bytes 27656 | tf_op jit(solution)/shard_map/ppermute | solution.py:21
  152.6 17.9 %collective-permute-start.9 = (bf16[2,18,34,128]{3,1,2,0:T(8,128)(2,1)}, bf16[2,18,34,128]{3,1,2,0:T(8,128)(2,1)}, u32[]{:S(2)}, u32[]{:S(2)}) collective-permute-start(bf16[2,18,34,128]{3,1,2,0:T(8,128)(2,1)} %pad_maximum_fusion.1), channel_id=1, source_target_pairs={{0,8},{8,16},{16,24},{1,9},{9,17},{17,25},{2,10},{10,18},{18,26},{... | collective-permute-start | bytes 940040 | tf_op jit(solution)/shard_map/ppermute | solution.py:33
  169.0 13.0 %collective-permute-start.19 = (bf16[2,18,34,128]{3,1,2,0:T(8,128)(2,1)}, bf16[2,18,34,128]{3,1,2,0:T(8,128)(2,1)}, u32[]{:S(2)}, u32[]{:S(2)}) collective-permute-start(bf16[2,18,34,128]{3,1,2,0:T(8,128)(2,1)} %pad_maximum_fusion.2), channel_id=1, source_target_pairs={{8,0},{16,8},{24,16},{9,1},{17,9},{25,17},{10,2},{18,10},{26,18},{... | collective-permute-start | bytes 940040 | tf_op jit(solution)/shard_map/ppermute | solution.py:33
  (25 other events, 259.3 us)
Sparse Core Ops, SparseCore 0:
  181.9 141.6 all-reduce.4
where the time goes:
time: 335 us; the launch traced here: 334 us
  waiting for transfers between devices  117 us (35%)
  blocking collectives  92 us (27%)
  starting transfers between devices  53.2 us (16%)
  matrix products  27.9 us (8%)
  other arithmetic  18.4 us (5%)
  between operations  14.9 us (4%)
  local copies, waits for them, and re-layouts  10.5 us (3%)
    psum x1, waiting for transfers between devices, on_device(): lax.psum((first_term, second_term), ('tm', 'row', 'col'))  114 us
    psum x2, blocking collectives, norm_act(): group_mean = lax.psum(group_sum(values), ('row', 'col')) / count  33.1 us
    ppermute x8, starting transfers between devices, extended(): lax.ppermute(tail, axis, [(i, (i + 1) % count) for i in range(ends)])  30.9 us
    psum x2, blocking collectives, norm_back(): lax.psum((group_sum(grad_norm), group_sum(grad_norm * normed)), ('row', '...  30.2 us
    psum x2, blocking collectives, norm_act(): spread = lax.psum(group_sum(centred * centred), ('row', 'col')) / count  28.7 us
    transpose x2, matrix products, weight_grad(): return jnp.transpose(summed, (1, 2, 3, 4, 0))  18 us
    ppermute x4, starting transfers between devices, passed_along(): return lax.ppermute(shard, axis, pairs)  11.8 us
    ppermute x8, starting transfers between devices, extended(): lax.ppermute(head, axis, [((i + 1) % count, i) for i in range(ends)])  10.5 us
  transfers between devices with their start and end apart: 21, of which 5 were waited for; matrix products, arithmetic and copies ran while one was open for 12% of the time, Pallas kernels for 0%

commit v1 on v0

--- a/solution.py
+++ b/solution.py
@@ -143,7 +143,7 @@
     feature_grad = (
         out_grad.astype(jnp.float32) + norm_back(grad_act1, norm_first, std_first)
     ).astype(jnp.bfloat16)
-    first_total, second_total = lax.psum((first_term, second_term), ("tm", "row", "col"))
+    first_total, second_total = lax.psum(lax.psum((first_term, second_term), ("row", "col")), "tm")
     first_grad = (first_total * factor).astype(jnp.bfloat16)
     second_grad = (second_total * factor).astype(jnp.bfloat16)
     return (result, feature_grad, first_grad, second_grad)

time: 335 us -> 402 us (1.20)
  waiting for transfers between devices: 117 us -> 188 us
    psum x1 -> x2, waiting for transfers between devices: 114 us -> 150 us  [the longest x1 76.5 us: on_device(): lax.psum((first_term, second_term), ('row', 'col'))]
    ppermute x4, waiting for transfers between devices: 0.16 us -> 31 us  [passed_along(): return lax.ppermute(shard, axis, pairs)]
  transfers between devices with their start and end apart: 21 -> 22, of which waited for: 5 -> 9; matrix products, arithmetic and copies ran while one was open for 12% -> 6% of each run, Pallas kernels for 0% -> 0%
where the time goes in v1:
time: 402 us; the launch traced here: 401 us
  waiting for transfers between devices  188 us (47%)
  blocking collectives  91.9 us (23%)
  starting transfers between devices  51.7 us (13%)
  matrix products  28.2 us (7%)
  other arithmetic  15.8 us (4%)
  between operations  14.8 us (4%)
  local copies, waits for them, and re-layouts  10.2 us (3%)
    psum x1, waiting for transfers between devices, on_device(): lax.psum((first_term, second_term), ('row', 'col'))  76.5 us
    psum x1, waiting for transfers between devices, on_device(): lax.psum(lax.psum((first_term, second_term), ('row', 'col')), 'tm')  73.9 us
    psum x2, blocking collectives, norm_act(): group_mean = lax.psum(group_sum(values), ('row', 'col')) / count  33.1 us
    ppermute x4, waiting for transfers between devices, passed_along(): return lax.ppermute(shard, axis, pairs)  31 us
    psum x2, blocking collectives, norm_back(): lax.psum((group_sum(grad_norm), group_sum(grad_norm * normed)), ('row', '...  30.1 us
    ppermute x8, starting transfers between devices, extended(): lax.ppermute(tail, axis, [(i, (i + 1) % count) for i in range(ends)])  29.7 us
    psum x2, blocking collectives, norm_act(): spread = lax.psum(group_sum(centred * centred), ('row', 'col')) / count  28.7 us
    transpose x2, matrix products, weight_grad(): return jnp.transpose(summed, (1, 2, 3, 4, 0))  18.2 us
  transfers between devices with their start and end apart: 22, of which 9 were waited for; matrix products, arithmetic and copies ran while one was open for 6% of the time, Pallas kernels for 0%

profile of v1, /device:TPU:0, one launch (start us, length us, event | category | flops | bytes accessed | tf_op | source)
XLA Modules:
  0.0 400.7 jit_solution(509103014287984524)
XLA Ops:
  8.6 15.8 %psum.84 = f32[2,32]{1,0:T(2,128)S(1)} all-reduce(f32[2,32]{1,0:T(2,128)S(1)} %reduce_sum.145), channel_id=1, replica_groups=mesh['tm'=4,'row'=2,'col'=4] {'row','col'}, use_global_device_ids=true, to_apply=%region_2.0 | all-reduce | flops 64 | bytes 512 | tf_op jit(solution)/shard_map/psum | solution.py:86
  25.8 14.2 %psum.85 = f32[2,32]{1,0:T(2,128)S(1)} all-reduce(f32[2,32]{1,0:T(2,128)S(1)} %reduce_sum.147), channel_id=1, replica_groups=mesh['tm'=4,'row'=2,'col'=4] {'row','col'}, use_global_device_ids=true, to_apply=%region_5.0 | all-reduce | flops 64 | bytes 512 | tf_op jit(solution)/shard_map/psum | solution.py:88
  42.7 3.0 collective-permute-start
  50.4 4.8 %collective-permute-start.2 = (bf16[2,18,1,128]{3,1,2,0:T(8,128)(2,1)S(1)}, bf16[2,18,1,128]{3,1,2,0:T(8,128)(2,1)S(1)}, u32[]{:S(2)}, u32[]{:S(2)}) collective-permute-start(bf16[2,18,1,128]{3,1,2,0:T(8,128)(2,1)S(1)} %get-tuple-element.32), channel_id=1, source_target_pairs={{0,1},{1,2},{2,3},{4,5},{5,6},{6,7},{8,9},{9,10},{10,11},{12,13},{... | collective-permute-start | bytes 27656 | tf_op jit(solution)/shard_map/ppermute | solution.py:21
  56.9 3.5 collective-permute-start.4
  61.7 5.4 %collective-permute-start.12 = (bf16[2,18,1,128]{3,2,1,0:T(2,128)(2,1)S(1)}, bf16[2,18,1,128]{3,2,1,0:T(2,128)(2,1)S(1)}, u32[]{:S(2)}, u32[]{:S(2)}) collective-permute-start(bf16[2,18,1,128]{3,2,1,0:T(2,128)(2,1)S(1)} %get-tuple-element.34), channel_id=1, source_target_pairs={{0,1},{1,2},{2,3},{4,5},{5,6},{6,7},{8,9},{9,10},{10,11},{12,13},{... | collective-permute-start | bytes 27656 | tf_op jit(solution)/shard_map/ppermute | solution.py:21
  74.7 17.4 %psum.86 = f32[2,32]{1,0:T(2,128)S(1)} all-reduce(f32[2,32]{1,0:T(2,128)S(1)} %reduce_sum.149), channel_id=1, replica_groups=mesh['tm'=4,'row'=2,'col'=4] {'row','col'}, use_global_device_ids=true, to_apply=%region_8.0 | all-reduce | flops 64 | bytes 512 | tf_op jit(solution)/shard_map/psum | solution.py:86
  92.6 14.5 %psum.87 = f32[2,32]{1,0:T(2,128)S(1)} all-reduce(f32[2,32]{1,0:T(2,128)S(1)} %reduce_sum.151), channel_id=1, replica_groups=mesh['tm'=4,'row'=2,'col'=4] {'row','col'}, use_global_device_ids=true, to_apply=%region_11.0 | all-reduce | flops 64 | bytes 512 | tf_op jit(solution)/shard_map/psum | solution.py:88
  109.0 2.5 convolution_select_fusion.1
  112.3 14.7 %all-reduce.1 = (f32[2,32]{1,0:T(2,128)S(1)}, f32[2,32]{1,0:T(2,128)S(1)}) all-reduce(f32[2,32]{1,0:T(2,128)S(1)} %reduce_sum.155, f32[2,32]{1,0:T(2,128)S(1)} %reduce_sum.153), channel_id=1, replica_groups=mesh['tm'=4,'row'=2,'col'=4] {'row','col'}, use_global_device_ids=true, to_apply=%region_17.18 | all-reduce | flops 128 | bytes 1024 | tf_op jit(solution)/shard_map/psum | solution.py:99
  129.8 3.0 collective-permute-start.5
  135.0 4.5 %collective-permute-start.7 = (bf16[2,18,1,128]{3,1,2,0:T(8,128)(2,1)S(1)}, bf16[2,18,1,128]{3,1,2,0:T(8,128)(2,1)S(1)}, u32[]{:S(2)}, u32[]{:S(2)}) collective-permute-start(bf16[2,18,1,128]{3,1,2,0:T(8,128)(2,1)S(1)} %get-tuple-element.30), channel_id=1, source_target_pairs={{0,1},{1,2},{2,3},{4,5},{5,6},{6,7},{8,9},{9,10},{10,11},{12,13},{... | collective-permute-start | bytes 27656 | tf_op jit(solution)/shard_map/ppermute | solution.py:21
  141.9 5.3 %collective-permute-start.9 = (bf16[2,18,34,128]{3,1,2,0:T(8,128)(2,1)}, bf16[2,18,34,128]{3,1,2,0:T(8,128)(2,1)}, u32[]{:S(2)}, u32[]{:S(2)}) collective-permute-start(bf16[2,18,34,128]{3,1,2,0:T(8,128)(2,1)} %pad_maximum_fusion.1), channel_id=1, source_target_pairs={{0,8},{8,16},{16,24},{1,9},{9,17},{17,25},{2,10},{10,18},{18,26},{... | collective-permute-start | bytes 940040 | tf_op jit(solution)/shard_map/ppermute | solution.py:33
  147.3 9.0 %fusion.6 = f32[3,3,3,128,128]{4,3,2,1,0:T(8,128)} fusion(bf16[1,4,18,34,128]{4,2,3,1,0:T(8,128)(2,1)S(1)} %copy-done.9, bf16[2,16,32,1,128]{4,1,2,0,3:T(8,128)(2,1)S(1)} %fusion.67), kind=kOutput, calls=%fused_computation.9 | convolution fusion | flops 905969664 | bytes 2658304 | tf_op jit(solution)/shard_map/transpose | solution.py:116
  158.6 9.2 %fusion.4 = f32[3,3,3,128,128]{4,3,2,1,0:T(8,128)} fusion(bf16[1,4,18,34,128]{4,2,3,1,0:T(8,128)(2,1)S(1)} %get-tuple-element.22, bf16[2,16,32,1,128]{4,2,1,0,3:T(8,128)(2,1)S(1)} %bitcast.93), kind=kOutput, calls=%fused_computation.7 | convolution fusion | flops 905969664 | bytes 2658304 | tf_op jit(solution)/shard_map/transpose | solution.py:116
  167.9 76.5 %all-reduce.7.cloned.1.call-done = (f32[3,3,3,128,128]{4,3,2,1,0:T(8,128)}, f32[3,3,3,128,128]{4,3,2,1,0:T(8,128)}) async-done(((f32[3,3,3,128,128]{4,3,2,1,0:T(8,128)}, f32[3,3,3,128,128]{4,3,2,1,0:T(8,128)}), (f32[3,3,3,128,128]{4,3,2,1,0:T(8,128)}, f32[3,3,3,128,128]{4,3,2,1,0:T(8,128)})) %all-reduce.7.cloned.1.call-update) | async-done | bytes 3538960 | tf_op jit(solution)/shard_map/psum | solution.py:146
  246.7 3.0 collective-permute-start.15
  251.9 4.5 %collective-permute-start.17 = (bf16[2,18,1,128]{3,1,2,0:T(8,128)(2,1)S(1)}, bf16[2,18,1,128]{3,1,2,0:T(8,128)(2,1)S(1)}, u32[]{:S(2)}, u32[]{:S(2)}) collective-permute-start(bf16[2,18,1,128]{3,1,2,0:T(8,128)(2,1)S(1)} %get-tuple-element.28), channel_id=1, source_target_pairs={{0,1},{1,2},{2,3},{4,5},{5,6},{6,7},{8,9},{9,10},{10,11},{12,13},{... | collective-permute-start | bytes 27656 | tf_op jit(solution)/shard_map/ppermute | solution.py:21
  259.4 31.0 %collective-permute-done.19 = bf16[2,18,34,128]{3,1,2,0:T(8,128)(2,1)S(1)} collective-permute-done((bf16[2,18,34,128]{3,1,2,0:T(8,128)(2,1)S(1)}, bf16[2,18,34,128]{3,1,2,0:T(8,128)(2,1)S(1)}, u32[]{:S(2)}, u32[]{:S(2)}) %collective-permute-start.19) | collective-permute-done | bytes 313376 | tf_op jit(solution)/shard_map/ppermute | solution.py:33
  291.3 2.5 convolution_select_fusion
  294.7 15.3 %all-reduce = (f32[2,32]{1,0:T(2,128)S(1)}, f32[2,32]{1,0:T(2,128)S(1)}) all-reduce(f32[2,32]{1,0:T(2,128)S(1)} %reduce_sum.159, f32[2,32]{1,0:T(2,128)S(1)} %reduce_sum.157), channel_id=1, replica_groups=mesh['tm'=4,'row'=2,'col'=4] {'row','col'}, use_global_device_ids=true, to_apply=%region_23.24 | all-reduce | flops 128 | bytes 1024 | tf_op jit(solution)/shard_map/psum | solution.py:99
  311.6 2.5 convolution_select_fusion.2
  316.1 73.9 %all-reduce.9.cloned.1.call-done = (f32[3,3,3,128,128]{4,3,2,1,0:T(8,128)}, f32[3,3,3,128,128]{4,3,2,1,0:T(8,128)}) async-done(((f32[3,3,3,128,128]{4,3,2,1,0:T(8,128)}, f32[3,3,3,128,128]{4,3,2,1,0:T(8,128)}), (f32[3,3,3,128,128]{4,3,2,1,0:T(8,128)}, f32[3,3,3,128,128]{4,3,2,1,0:T(8,128)})) %all-reduce.9.cloned.1.call-update) | async-done | bytes 3538960 | tf_op jit(solution)/shard_map/psum | solution.py:146
  390.0 2.8 multiply_convert_fusion.1
  (171 shorter events, 46.9 us)
Async XLA Ops:
  7.2 64.5 %copy-start = (bf16[3,3,3,128,128]{4,3,2,1,0:T(8,128)(2,1)S(1)}, bf16[3,3,3,128,128]{4,3,2,1,0:T(8,128)(2,1)}, u32[]{:S(2)}) copy-start(bf16[3,3,3,128,128]{4,3,2,1,0:T(8,128)(2,1)} %param.5) | copy-start | bytes 2654212
  7.2 48.1 %copy-start.7 = (bf16[2,16,32,128]{3,2,1,0:T(8,128)(2,1)S(1)}, bf16[2,16,32,128]{3,2,1,0:T(8,128)(2,1)}, u32[]{:S(2)}) copy-start(bf16[2,16,32,128]{3,2,1,0:T(8,128)(2,1)} %param.7) | copy-start | bytes 786436
  7.2 237.2 %all-reduce.7.cloned.1.call-start = ((), (), s32[]{:S(2)}) async-start(), calls=%async_computation | async-start | bytes 7077888 | tf_op jit(solution)/shard_map/psum | solution.py:146
  41.4 7.7 %collective-permute-start.1 = (bf16[2,1,32,128]{3,1,2,0:T(2,128)(2,1)S(1)}, bf16[2,1,32,128]{3,1,2,0:T(2,128)(2,1)S(1)}, u32[]{:S(2)}, u32[]{:S(2)}) collective-permute-start(bf16[2,1,32,128]{3,1,2,0:T(2,128)(2,1)S(1)} %get-tuple-element.45), channel_id=1, source_target_pairs={{4,0},{5,1},{6,2},{7,3},{12,8},{13,9},{14,10},{15,11},{20,16},{21,... | collective-permute-start | bytes 49160 | tf_op jit(solution)/shard_map/ppermute | solution.py:23
  42.7 6.4 %collective-permute-start = (bf16[2,1,32,128]{3,1,2,0:T(2,128)(2,1)S(1)}, bf16[2,1,32,128]{3,1,2,0:T(2,128)(2,1)S(1)}, u32[]{:S(2)}, u32[]{:S(2)}) collective-permute-start(bf16[2,1,32,128]{3,1,2,0:T(2,128)(2,1)S(1)} %get-tuple-element.44), channel_id=1, source_target_pairs={{0,4},{1,5},{2,6},{3,7},{8,12},{9,13},{10,14},{11,15},{16,20},{17,... | collective-permute-start | bytes 49160 | tf_op jit(solution)/shard_map/ppermute | solution.py:21
  46.5 8.8 %collective-permute-start.10 = (bf16[2,1,32,128]{3,2,1,0:T(8,128)(2,1)S(1)}, bf16[2,1,32,128]{3,2,1,0:T(8,128)(2,1)S(1)}, u32[]{:S(2)}, u32[]{:S(2)}) collective-permute-start(bf16[2,1,32,128]{3,2,1,0:T(8,128)(2,1)S(1)} %get-tuple-element.41), channel_id=1, source_target_pairs={{0,4},{1,5},{2,6},{3,7},{8,12},{9,13},{10,14},{11,15},{16,20},{17,... | collective-permute-start | bytes 49160 | tf_op jit(solution)/shard_map/ppermute | solution.py:21
  47.8 7.5 %collective-permute-start.11 = (bf16[2,1,32,128]{3,2,1,0:T(8,128)(2,1)S(1)}, bf16[2,1,32,128]{3,2,1,0:T(8,128)(2,1)S(1)}, u32[]{:S(2)}, u32[]{:S(2)}) collective-permute-start(bf16[2,1,32,128]{3,2,1,0:T(8,128)(2,1)S(1)} %get-tuple-element.40), channel_id=1, source_target_pairs={{4,0},{5,1},{6,2},{7,3},{12,8},{13,9},{14,10},{15,11},{20,16},{21,... | collective-permute-start | bytes 49160 | tf_op jit(solution)/shard_map/ppermute | solution.py:23
  49.1 6.2 %collective-permute-start.3 = (bf16[2,18,1,128]{3,1,2,0:T(8,128)(2,1)S(1)}, bf16[2,18,1,128]{3,1,2,0:T(8,128)(2,1)S(1)}, u32[]{:S(2)}, u32[]{:S(2)}) collective-permute-start(bf16[2,18,1,128]{3,1,2,0:T(8,128)(2,1)S(1)} %get-tuple-element.33), channel_id=1, source_target_pairs={{1,0},{2,1},{3,2},{5,4},{6,5},{7,6},{9,8},{10,9},{11,10},{13,12},{... | collective-permute-start | bytes 27656 | tf_op jit(solution)/shard_map/ppermute | solution.py:23
  50.4 6.2 %collective-permute-start.2 = (bf16[2,18,1,128]{3,1,2,0:T(8,128)(2,1)S(1)}, bf16[2,18,1,128]{3,1,2,0:T(8,128)(2,1)S(1)}, u32[]{:S(2)}, u32[]{:S(2)}) collective-permute-start(bf16[2,18,1,128]{3,1,2,0:T(8,128)(2,1)S(1)} %get-tuple-element.32), channel_id=1, source_target_pairs={{0,1},{1,2},{2,3},{4,5},{5,6},{6,7},{8,9},{9,10},{10,11},{12,13},{... | collective-permute-start | bytes 27656 | tf_op jit(solution)/shard_map/ppermute | solution.py:21
  56.9 13.2 %collective-permute-start.4 = (bf16[2,18,34,128]{3,1,2,0:T(8,128)(2,1)S(1)}, bf16[2,18,34,128]{3,1,2,0:T(8,128)(2,1)S(1)}, u32[]{:S(2)}, u32[]{:S(2)}) collective-permute-start(bf16[2,18,34,128]{3,1,2,0:T(8,128)(2,1)S(1)} %pad_maximum_fusion), channel_id=1, source_target_pairs={{0,8},{8,16},{16,24},{1,9},{9,17},{17,25},{2,10},{10,18},{18,26},{... | collective-permute-start | bytes 940040 | tf_op jit(solution)/shard_map/ppermute | solution.py:33
  60.4 6.8 %collective-permute-start.13 = (bf16[2,18,1,128]{3,2,1,0:T(2,128)(2,1)S(1)}, bf16[2,18,1,128]{3,2,1,0:T(2,128)(2,1)S(1)}, u32[]{:S(2)}, u32[]{:S(2)}) collective-permute-start(bf16[2,18,1,128]{3,2,1,0:T(2,128)(2,1)S(1)} %get-tuple-element.35), channel_id=1, source_target_pairs={{1,0},{2,1},{3,2},{5,4},{6,5},{7,6},{9,8},{10,9},{11,10},{13,12},{... | collective-permute-start | bytes 27656 | tf_op jit(solution)/shard_map/ppermute | solution.py:23
  61.7 6.9 %collective-permute-start.12 = (bf16[2,18,1,128]{3,2,1,0:T(2,128)(2,1)S(1)}, bf16[2,18,1,128]{3,2,1,0:T(2,128)(2,1)S(1)}, u32[]{:S(2)}, u32[]{:S(2)}) collective-permute-start(bf16[2,18,1,128]{3,2,1,0:T(2,128)(2,1)S(1)} %get-tuple-element.34), channel_id=1, source_target_pairs={{0,1},{1,2},{2,3},{4,5},{5,6},{6,7},{8,9},{9,10},{10,11},{12,13},{... | collective-permute-start | bytes 27656 | tf_op jit(solution)/shard_map/ppermute | solution.py:21
  68.8 38.5 %collective-permute-start.14 = (bf16[2,18,34,128]{3,2,1,0:T(8,128)(2,1)S(1)}, bf16[2,18,34,128]{3,2,1,0:T(8,128)(2,1)S(1)}, u32[]{:S(2)}, u32[]{:S(2)}) collective-permute-start(bf16[2,18,34,128]{3,2,1,0:T(8,128)(2,1)S(1)} %pad_maximum_fusion.3), channel_id=1, source_target_pairs={{8,0},{16,8},{24,16},{9,1},{17,9},{25,17},{10,2},{18,10},{26,18},{... | collective-permute-start | bytes 940040 | tf_op jit(solution)/shard_map/ppermute | solution.py:33
  128.4 4.5 %collective-permute-start.6 = (bf16[2,1,32,128]{3,1,2,0:T(2,128)(2,1)S(1)}, bf16[2,1,32,128]{3,1,2,0:T(2,128)(2,1)S(1)}, u32[]{:S(2)}, u32[]{:S(2)}) collective-permute-start(bf16[2,1,32,128]{3,1,2,0:T(2,128)(2,1)S(1)} %get-tuple-element.43), channel_id=1, source_target_pairs={{4,0},{5,1},{6,2},{7,3},{12,8},{13,9},{14,10},{15,11},{20,16},{21,... | collective-permute-start | bytes 49160 | tf_op jit(solution)/shard_map/ppermute | solution.py:23
  129.8 3.9 collective-permute-start.5
  133.7 6.2 %collective-permute-start.8 = (bf16[2,18,1,128]{3,1,2,0:T(8,128)(2,1)S(1)}, bf16[2,18,1,128]{3,1,2,0:T(8,128)(2,1)S(1)}, u32[]{:S(2)}, u32[]{:S(2)}) collective-permute-start(bf16[2,18,1,128]{3,1,2,0:T(8,128)(2,1)S(1)} %get-tuple-element.31), channel_id=1, source_target_pairs={{1,0},{2,1},{3,2},{5,4},{6,5},{7,6},{9,8},{10,9},{11,10},{13,12},{... | collective-permute-start | bytes 27656 | tf_op jit(solution)/shard_map/ppermute | solution.py:23
  135.0 5.9 %collective-permute-start.7 = (bf16[2,18,1,128]{3,1,2,0:T(8,128)(2,1)S(1)}, bf16[2,18,1,128]{3,1,2,0:T(8,128)(2,1)S(1)}, u32[]{:S(2)}, u32[]{:S(2)}) collective-permute-start(bf16[2,18,1,128]{3,1,2,0:T(8,128)(2,1)S(1)} %get-tuple-element.30), channel_id=1, source_target_pairs={{0,1},{1,2},{2,3},{4,5},{5,6},{6,7},{8,9},{9,10},{10,11},{12,13},{... | collective-permute-start | bytes 27656 | tf_op jit(solution)/shard_map/ppermute | solution.py:21
  141.9 14.4 %collective-permute-start.9 = (bf16[2,18,34,128]{3,1,2,0:T(8,128)(2,1)}, bf16[2,18,34,128]{3,1,2,0:T(8,128)(2,1)}, u32[]{:S(2)}, u32[]{:S(2)}) collective-permute-start(bf16[2,18,34,128]{3,1,2,0:T(8,128)(2,1)} %pad_maximum_fusion.1), channel_id=1, source_target_pairs={{0,8},{8,16},{16,24},{1,9},{9,17},{17,25},{2,10},{10,18},{18,26},{... | collective-permute-start | bytes 940040 | tf_op jit(solution)/shard_map/ppermute | solution.py:33
  167.8 222.1 %all-reduce.9.cloned.1.call-start = ((), (), s32[]{:S(2)}) async-start(), calls=%async_computation.1 | async-start | bytes 7077888 | tf_op jit(solution)/shard_map/psum | solution.py:146
  245.4 4.3 %collective-permute-start.16 = (bf16[2,1,32,128]{3,1,2,0:T(2,128)(2,1)S(1)}, bf16[2,1,32,128]{3,1,2,0:T(2,128)(2,1)S(1)}, u32[]{:S(2)}, u32[]{:S(2)}) collective-permute-start(bf16[2,1,32,128]{3,1,2,0:T(2,128)(2,1)S(1)} %get-tuple-element.39), channel_id=1, source_target_pairs={{4,0},{5,1},{6,2},{7,3},{12,8},{13,9},{14,10},{15,11},{20,16},{21,... | collective-permute-start | bytes 49160 | tf_op jit(solution)/shard_map/ppermute | solution.py:23
  246.7 3.9 collective-permute-start.15
  250.6 5.9 %collective-permute-start.18 = (bf16[2,18,1,128]{3,1,2,0:T(8,128)(2,1)S(1)}, bf16[2,18,1,128]{3,1,2,0:T(8,128)(2,1)S(1)}, u32[]{:S(2)}, u32[]{:S(2)}) collective-permute-start(bf16[2,18,1,128]{3,1,2,0:T(8,128)(2,1)S(1)} %get-tuple-element.29), channel_id=1, source_target_pairs={{1,0},{2,1},{3,2},{5,4},{6,5},{7,6},{9,8},{10,9},{11,10},{13,12},{... | collective-permute-start | bytes 27656 | tf_op jit(solution)/shard_map/ppermute | solution.py:23
  251.9 5.9 %collective-permute-start.17 = (bf16[2,18,1,128]{3,1,2,0:T(8,128)(2,1)S(1)}, bf16[2,18,1,128]{3,1,2,0:T(8,128)(2,1)S(1)}, u32[]{:S(2)}, u32[]{:S(2)}) collective-permute-start(bf16[2,18,1,128]{3,1,2,0:T(8,128)(2,1)S(1)} %get-tuple-element.28), channel_id=1, source_target_pairs={{0,1},{1,2},{2,3},{4,5},{5,6},{6,7},{8,9},{9,10},{10,11},{12,13},{... | collective-permute-start | bytes 27656 | tf_op jit(solution)/shard_map/ppermute | solution.py:21
  258.1 32.3 %collective-permute-start.19 = (bf16[2,18,34,128]{3,1,2,0:T(8,128)(2,1)S(1)}, bf16[2,18,34,128]{3,1,2,0:T(8,128)(2,1)S(1)}, u32[]{:S(2)}, u32[]{:S(2)}) collective-permute-start(bf16[2,18,34,128]{3,1,2,0:T(8,128)(2,1)S(1)} %pad_maximum_fusion.2), channel_id=1, source_target_pairs={{8,0},{16,8},{24,16},{9,1},{17,9},{25,17},{10,2},{18,10},{26,18},{... | collective-permute-start | bytes 940040 | tf_op jit(solution)/shard_map/ppermute | solution.py:33
  (22 other events, 155.3 us)
Sparse Core Ops, SparseCore 0:
  167.9 76.4 all-reduce.6
  246.8 143.0 all-reduce.8
